TPU v7x, 128 devices: a whole 4x4x4 slice. The times are simulated.
128 devices in a mesh: row: 8 (over x, core), col: 16 (over z, y).
Axes of the slice: x: 4, y: 4, z: 4, core: 2. Of those that a mesh axis runs over, the one named last changes fastest.
Arguments:
- features: float32 [32768, 128], P('col', 'row'), may hold values from -6 to 6
- tile_rows: int32 [8, 16, 80], P('row', 'col'), may hold values from 0 to 32, as said below
- tile_cols: int32 [8, 16, 80], P('row', 'col'), may hold values from 0 to 15
- tile_values: float32 [8, 16, 80, 128, 128], P('row', 'col'), may hold values from -0.51881118 to 0.51881118, as said below
- weight_in: float32 [128, 256], replicated, may hold values from -0.5 to 0.5
- weight_out: float32 [256, 256], replicated, may hold values from -0.375 to 0.375
- cotangent: float32 [32768, 256], P(('col', 'row')), may hold values from -0.03125 to 0.03125
Outputs:
- output: float32 [32768, 256], P(('col', 'row'))
- grad_in: float32 [128, 256], replicated
- grad_out: float32 [256, 256], replicated
Inputs may be any that keep to these rules, and one draw needn't show every extreme that they name: `tile_rows`: slot s of device (i, j) is used for s below that device's tile count and holds a tile row 0 to 31; unused slots hold 32. Used slots come first, no (row, column) pair repeats within a device, and in every draw some device uses all 80 slots. `tile_values`: A tile is sparse: each entry is nonzero with probability 2.56 / 128, at random positions.
All inputs are finite; a program needn't handle non-finite values.
Results may differ from a plain program's by a relative error of at most 0.0003.
Values sent between devices are 32-bit elements; how exact they have to be, the bound alone decides.
A program may use at most 128 MiB of HBM per device.

v0:
```python
import jax
import jax.numpy as jnp
from jax import lax
from jax.sharding import PartitionSpec as P

TILE = 128


def forward_tiles(gathered, tile_row, tile_col, tile_block, out_tiles):
    width = gathered.shape[1]
    blocks = gathered.reshape(-1, TILE, width)
    picked = jnp.take(blocks, tile_col, axis=0)
    products = jnp.einsum("tab,tbf->taf", tile_block, picked, precision=lax.Precision.HIGHEST)
    onehot = (tile_row[None, :] == jnp.arange(out_tiles, dtype=jnp.int32)[:, None]).astype(
        jnp.float32
    )
    summed = jnp.einsum("rt,taf->raf", onehot, products, precision=lax.Precision.HIGHEST)
    return summed.reshape(out_tiles * TILE, width)


def adjoint_tiles(row_grads, tile_row, tile_col, tile_block, out_tiles):
    width = row_grads.shape[1]
    in_tiles = row_grads.shape[0] // TILE
    blocks = row_grads.reshape(in_tiles, TILE, width)
    picked = jnp.take(blocks, jnp.minimum(tile_row, in_tiles - 1), axis=0)
    products = jnp.einsum("tba,tbf->taf", tile_block, picked, precision=lax.Precision.HIGHEST)
    matches = tile_col[None, :] == jnp.arange(out_tiles, dtype=jnp.int32)[:, None]
    onehot = (matches & (tile_row < in_tiles)[None, :]).astype(jnp.float32)
    summed = jnp.einsum("rt,taf->raf", onehot, products, precision=lax.Precision.HIGHEST)
    return summed.reshape(out_tiles * TILE, width)


def dense_product(left, right):
    return jnp.dot(left, right, precision=lax.Precision.HIGHEST, preferred_element_type=jnp.float32)


def inner_rows(left, right):
    return lax.dot_general(
        left,
        right,
        (((0,), (0,)), ((), ())),
        precision=lax.Precision.HIGHEST,
        preferred_element_type=jnp.float32,
    )


def per_device(features, tile_rows, tile_cols, tile_values, weight_in, weight_out, cotangent):
    tile_row = tile_rows.reshape(-1)
    tile_col = tile_cols.reshape(-1)
    tile_block = tile_values.reshape(-1, TILE, TILE)
    local_rows = cotangent.shape[0]
    row_tiles = lax.axis_size("col") * local_rows // TILE
    col_tiles = lax.axis_size("row") * local_rows // TILE
    x_local = lax.all_to_all(features, "row", split_axis=0, concat_axis=1, tiled=True)
    support = dense_product(x_local, weight_in)
    gathered = lax.all_gather(support, "row", axis=0, tiled=True)
    partial_one = forward_tiles(gathered, tile_row, tile_col, tile_block, row_tiles)
    pre_act = lax.psum_scatter(partial_one, "col", scatter_dimension=0, tiled=True)
    hidden = jax.nn.silu(pre_act)
    support_two = dense_product(hidden, weight_out)
    gathered_two = lax.all_gather(support_two, "row", axis=0, tiled=True)
    partial_two = forward_tiles(gathered_two, tile_row, tile_col, tile_block, row_tiles)
    output = lax.psum_scatter(partial_two, "col", scatter_dimension=0, tiled=True)
    rows_out = lax.all_gather(cotangent, "col", axis=0, tiled=True)
    adjoint_two = adjoint_tiles(rows_out, tile_row, tile_col, tile_block, col_tiles)
    d_support_two = lax.psum_scatter(adjoint_two, "row", scatter_dimension=0, tiled=True)
    grad_out_local = inner_rows(hidden, d_support_two)
    d_hidden = dense_product(d_support_two, weight_out.T)
    sigmoid_pre = jax.nn.sigmoid(pre_act)
    d_pre = d_hidden * sigmoid_pre * (1.0 + pre_act * (1.0 - sigmoid_pre))
    rows_in = lax.all_gather(d_pre, "col", axis=0, tiled=True)
    adjoint_one = adjoint_tiles(rows_in, tile_row, tile_col, tile_block, col_tiles)
    d_support = lax.psum_scatter(adjoint_one, "row", scatter_dimension=0, tiled=True)
    grad_in_local = inner_rows(x_local, d_support)
    grad_in, grad_out = lax.psum((grad_in_local, grad_out_local), ("row", "col"))
    return (output, grad_in, grad_out)


def solution(mesh):
    return jax.shard_map(
        per_device,
        mesh=mesh,
        in_specs=(
            P("col", "row"),
            P("row", "col", None),
            P("row", "col", None),
            P("row", "col", None, None, None),
            P(),
            P(),
            P(("col", "row"), None),
        ),
        out_specs=(P(("col", "row"), None), P(), P()),
        check_vma=False,
    )
```

profile of v0, /device:TPU:0, one launch (start us, length us, event | category | flops | bytes accessed | tf_op | source)
XLA Modules:
  0.0 643.5 jit_solution(13298213714380566996)
XLA Ops:
  8.9 10.3 %all_to_all.19 = f32[8,256,16]{1,2,0:T(8,128)S(1)} all-to-all(f32[8,256,16]{1,2,0:T(8,128)S(1)} %bitcast.80), channel_id=1, replica_groups=mesh['row'=8,'col'=16] {'row'}, dimensions={0} | all-to-all | bytes 262144 | tf_op jit(solution)/shard_map/all_to_all | solution.py:54
  19.2 2.0 fusion.69
  22.0 42.2 %all-gather.9.cloned.1.call-done = f32[4096,256]{1,0:T(8,128)} async-done(((f32[256,256]{1,0:T(8,128)}), f32[4096,256]{1,0:T(8,128)}) %all-gather.9.cloned.1.call-update) | async-done | bytes 4194320 | tf_op jit(solution)/shard_map/all_gather | solution.py:64
  64.2 9.9 %gather_fusion.2 = f32[80,128,256]{2,1,0:T(8,128)} fusion(f32[32,128,256]{2,1,0:T(8,128)} %bitcast.72, s32[1024]{0:T(1024)S(1)} %pad_clamp_fusion), kind=kCustom, calls=%fused_computation.1.clone | custom fusion | bytes 20971840 | tf_op jit(solution)/shard_map/jit(_take)/gather | solution.py:25
  74.0 23.1 %fusion.30 = f32[80,128,256]{1,2,0:T(8,128)} fusion(f32[1,1,80,128,128]{4,3,2,1,0:T(8,128)} %param.14, f32[80,128,256]{2,1,0:T(8,128)} %gather_fusion.2, pred[80]{0:T(512)(128)(4,1)S(1)} %get-tuple-element.22), kind=kOutput, calls=%fused_computation.26 | convolution fusion | flops 4029153280 | bytes 26214480 | tf_op jit(solution)/shard_map/tba,tbf->taf/dot_general | solution.py:26
  97.2 11.6 %copy.48 = f32[80,128,256]{2,0,1:T(8,128)} copy(f32[80,128,256]{1,2,0:T(8,128)} %fusion.30) | data formatting | bytes 20971520 | tf_op jit(solution)/shard_map/tba,tbf->taf/dot_general | solution.py:26
  108.8 6.2 fusion.57
  115.1 2.6 copy.49
  118.1 9.9 %gather_fusion = f32[80,128,256]{2,1,0:T(8,128)} fusion(f32[16,128,256]{2,1,0:T(8,128)} %bitcast.70, s32[1024]{0:T(1024)S(1)} %pad_clamp_fusion.1), kind=kCustom, calls=%fused_computation.clone | custom fusion | bytes 20971840 | tf_op jit(solution)/shard_map/jit(_take)/gather | solution.py:12
  128.0 23.0 %fusion.20 = f32[80,128,256]{1,2,0:T(8,128)} fusion(f32[1,1,80,128,128]{4,3,2,1,0:T(8,128)} %param.14, f32[80,128,256]{2,1,0:T(8,128)} %gather_fusion, pred[80]{0:T(512)(128)(4,1)S(1)} %compare_and_fusion.1), kind=kOutput, calls=%fused_computation.24 | convolution fusion | flops 4029153280 | bytes 26214480 | tf_op jit(solution)/shard_map/tab,tbf->taf/dot_general | solution.py:13
  151.0 11.7 %copy.42 = f32[80,128,256]{2,0,1:T(8,128)} copy(f32[80,128,256]{1,2,0:T(8,128)} %fusion.20) | data formatting | bytes 20971520 | tf_op jit(solution)/shard_map/tab,tbf->taf/dot_general | solution.py:13
  162.7 6.9 %fusion.49 = f32[32,128,256]{2,0,1:T(8,128)S(1)} fusion(f32[80,128,256]{2,0,1:T(8,128)} %copy.42, s32[80]{0:T(128)S(1)} %bitcast.82), kind=kOutput, calls=%fused_computation.39 | convolution fusion | flops 1006635520 | bytes 14680384 | tf_op jit(solution)/shard_map/rt,taf->raf/dot_general | solution.py:17
  169.6 4.4 copy.43
  174.0 78.6 %reduce-scatter.5.cloned.1.call-done = f32[256,256]{1,0:T(8,128)} async-done(((f32[4096,256]{1,0:T(8,128)}), f32[256,256]{1,0:T(8,128)}) %reduce-scatter.5.cloned.1.call-update) | async-done | bytes 262160 | tf_op jit(solution)/shard_map/reduce_scatter | solution.py:58
  252.6 2.1 fusion.40
  254.8 2.1 fusion.44
  257.0 48.8 %all-gather.11.cloned.1.call-done = f32[4096,256]{1,0:T(8,128)} async-done(((f32[256,256]{1,0:T(8,128)}), f32[4096,256]{1,0:T(8,128)}) %all-gather.11.cloned.1.call-update) | async-done | bytes 4194320 | tf_op jit(solution)/shard_map/all_gather | solution.py:71
  305.8 10.1 %gather_fusion.3 = f32[80,128,256]{2,1,0:T(8,128)} fusion(f32[32,128,256]{2,1,0:T(8,128)} %bitcast.73, s32[1024]{0:T(1024)S(1)} %pad_clamp_fusion), kind=kCustom, calls=%fused_computation.3.clone | custom fusion | bytes 20971840 | tf_op jit(solution)/shard_map/jit(_take)/gather | solution.py:25
  315.8 23.2 %fusion.35 = f32[80,128,256]{1,2,0:T(8,128)} fusion(f32[1,1,80,128,128]{4,3,2,1,0:T(8,128)} %param.14, f32[80,128,256]{2,1,0:T(8,128)} %gather_fusion.3, pred[80]{0:T(512)(128)(4,1)S(1)} %get-tuple-element.22), kind=kOutput, calls=%fused_computation.27 | convolution fusion | flops 4029153280 | bytes 26214480 | tf_op jit(solution)/shard_map/tba,tbf->taf/dot_general | solution.py:26
  339.1 11.6 %copy.51 = f32[80,128,256]{2,0,1:T(8,128)} copy(f32[80,128,256]{1,2,0:T(8,128)} %fusion.35) | data formatting | bytes 20971520 | tf_op jit(solution)/shard_map/tba,tbf->taf/dot_general | solution.py:26
  350.7 6.3 fusion.55
  357.0 2.6 copy.52
  361.2 9.8 %gather_fusion.1 = f32[80,128,256]{2,1,0:T(8,128)} fusion(f32[16,128,256]{2,1,0:T(8,128)} %bitcast.71, s32[1024]{0:T(1024)S(1)} %pad_clamp_fusion.1), kind=kCustom, calls=%fused_computation.2.clone | custom fusion | bytes 20971840 | tf_op jit(solution)/shard_map/jit(_take)/gather | solution.py:12
  371.0 23.0 %fusion.25 = f32[80,128,256]{1,2,0:T(8,128)} fusion(f32[1,1,80,128,128]{4,3,2,1,0:T(8,128)} %param.14, f32[80,128,256]{2,1,0:T(8,128)} %gather_fusion.1, pred[80]{0:T(512)(128)(4,1)S(1)} %compare_and_fusion.1), kind=kOutput, calls=%fused_computation.25 | convolution fusion | flops 4029153280 | bytes 26214480 | tf_op jit(solution)/shard_map/tab,tbf->taf/dot_general | solution.py:13
  394.0 11.6 %copy.45 = f32[80,128,256]{2,0,1:T(8,128)} copy(f32[80,128,256]{1,2,0:T(8,128)} %fusion.25) | data formatting | bytes 20971520 | tf_op jit(solution)/shard_map/tab,tbf->taf/dot_general | solution.py:13
  405.6 2.2 convolution_bitcast_fusion
  408.2 6.9 %fusion.47 = f32[32,128,256]{2,0,1:T(8,128)S(1)} fusion(f32[80,128,256]{2,0,1:T(8,128)} %copy.45, s32[80]{0:T(128)S(1)} %bitcast.83), kind=kOutput, calls=%fused_computation.38 | convolution fusion | flops 1006635520 | bytes 14680384 | tf_op jit(solution)/shard_map/rt,taf->raf/dot_general | solution.py:17
  415.1 4.4 copy.46
  419.4 134.7 %all-reduce.3.cloned.1.call-done = (f32[128,256]{0,1:T(8,128)}, f32[256,256]{1,0:T(8,128)}) async-done(((f32[128,256]{0,1:T(8,128)}, f32[256,256]{1,0:T(8,128)}), (f32[128,256]{0,1:T(8,128)}, f32[256,256]{1,0:T(8,128)})) %all-reduce.3.cloned.1.call-update) | async-done | bytes 393232 | tf_op jit(solution)/shard_map/psum | solution.py:75
  554.2 1.7 copy.53
  555.8 79.0 %reduce-scatter.7.cloned.1.call-done = f32[256,256]{1,0:T(8,128)} async-done(((f32[4096,256]{1,0:T(8,128)}), f32[256,256]{1,0:T(8,128)}) %reduce-scatter.7.cloned.1.call-update) | async-done | bytes 262160 | tf_op jit(solution)/shard_map/reduce_scatter | solution.py:63
  634.9 1.7 copy.63
  (41 shorter events, 5.0 us)
Async XLA Ops:
  7.2 245.4 %copy-start = (f32[256,256]{1,0:T(8,128)S(1)}, f32[256,256]{1,0:T(8,128)}, u32[]{:S(2)}) copy-start(f32[256,256]{1,0:T(8,128)} %param.16) | copy-start | bytes 786436
  7.2 57.0 %all-gather.9.cloned.1.call-start = ((), (), s32[]{:S(2)}) async-start(), calls=%async_computation.9 | async-start | bytes 4456448 | tf_op jit(solution)/shard_map/all_gather | solution.py:64
  7.9 110.2 %all-gather.5.cloned.1.call-start = ((), (), s32[]{:S(2)}) async-start(), calls=%async_computation.5 | async-start | bytes 2359296 | tf_op jit(solution)/shard_map/all_gather | solution.py:56
  21.2 152.8 %reduce-scatter.9.cloned.1.call-start = ((), (), s32[]{:S(2)}) async-start(), calls=%async_computation.10 | async-start | bytes 2359296 | tf_op jit(solution)/shard_map/reduce_scatter | solution.py:66
  97.2 11.7 %copy-start.3 = (s32[1,1,80]{2,1,0:T(1,128)S(1)}, s32[1,1,80]{2,1,0:T(1,128)}, u32[]{:S(2)}) copy-start(s32[1,1,80]{2,1,0:T(1,128)} %param.13) | copy-start | bytes 964
  117.7 134.9 %reduce-scatter.5.cloned.1.call-start = ((), (), s32[]{:S(2)}) async-start(), calls=%async_computation.6 | async-start | bytes 4456448 | tf_op jit(solution)/shard_map/reduce_scatter | solution.py:58
  151.0 11.7 %copy-start.2 = (s32[1,1,80]{2,1,0:T(1,128)S(1)}, s32[1,1,80]{2,1,0:T(1,128)}, u32[]{:S(2)}) copy-start(s32[1,1,80]{2,1,0:T(1,128)} %param.12) | copy-start | bytes 964
  174.0 131.8 %all-gather.11.cloned.1.call-start = ((), (), s32[]{:S(2)}) async-start(), calls=%async_computation.11 | async-start | bytes 4456448 | tf_op jit(solution)/shard_map/all_gather | solution.py:71
  254.8 106.4 %all-gather.7.cloned.1.call-start = ((), (), s32[]{:S(2)}) async-start(), calls=%async_computation.7 | async-start | bytes 2359296 | tf_op jit(solution)/shard_map/all_gather | solution.py:61
  256.9 148.7 %reduce-scatter.11.cloned.1.call-start = ((), (), s32[]{:S(2)}) async-start(), calls=%async_computation.12 | async-start | bytes 2359296 | tf_op jit(solution)/shard_map/reduce_scatter | solution.py:73
  350.7 9.2 %copy-start.4 = (f32[256,256]{1,0:T(8,128)S(1)}, f32[256,256]{1,0:T(8,128)}, u32[]{:S(2)}) copy-start(f32[256,256]{1,0:T(8,128)} %reduce-scatter.9.cloned.1.call-done) | copy-start | bytes 786436
  350.7 9.2 %copy-start.5 = (f32[256,256]{1,0:T(8,128)S(1)}, f32[256,256]{1,0:T(8,128)}, u32[]{:S(2)}) copy-start(f32[256,256]{1,0:T(8,128)} %reduce-scatter.5.cloned.1.call-done) | copy-start | bytes 786436
  359.6 194.6 %all-reduce.3.cloned.1.call-start = ((), (), s32[]{:S(2)}) async-start(), calls=%async_computation.13 | async-start | bytes 786432 | tf_op jit(solution)/shard_map/psum | solution.py:75
  407.9 228.7 %copy-start.1 = (f32[256,256]{1,0:T(8,128)S(1)}, f32[256,256]{1,0:T(8,128)}, u32[]{:S(2)}) copy-start(f32[256,256]{1,0:T(8,128)} %param.16) | copy-start | bytes 786436
  407.9 227.0 %reduce-scatter.7.cloned.1.call-start = ((), (), s32[]{:S(2)}) async-start(), calls=%async_computation.8 | async-start | bytes 4456448 | tf_op jit(solution)/shard_map/reduce_scatter | solution.py:63
Sparse Core Ops, SparseCore 0:
  10.1 53.9 all-gather.8
  66.5 24.8 all-gather.4
  117.8 33.6 reduce-scatter.8
  174.1 78.4 reduce-scatter.4
  255.1 50.5 all-gather.10
  307.9 24.8 all-gather.6
  359.7 33.6 reduce-scatter.10
  408.0 146.1 all-reduce.2
  558.1 76.7 reduce-scatter.6
where the time goes:
time: 653 us; the launch traced here: 644 us
  waiting for transfers between devices  384 us (59%)
  matrix products  128 us (20%)
  local copies, waits for them, and re-layouts  104 us (16%)
  between operations  14.4 us (2%)
  blocking collectives  10.3 us (2%)
    psum x1, waiting for transfers between devices, per_device(): lax.psum((grad_in_local, grad_out_local), ('row', 'col'))  135 us
    reduce_scatter x1, waiting for transfers between devices, per_device(): lax.psum_scatter(partial_two, 'col', scatter_dimension=0, tiled=True)  79 us
    reduce_scatter x1, waiting for transfers between devices, per_device(): lax.psum_scatter(partial_one, 'col', scatter_dimension=0, tiled=True)  78.6 us
    all_gather x1, waiting for transfers between devices, per_device(): rows_in = lax.all_gather(d_pre, 'col', axis=0, tiled=True)  48.8 us
    dot_general x2, matrix products, adjoint_tiles(): jnp.einsum('tba,tbf->taf', tile_block, picked, precision=lax.Precision.HI...  46.4 us
    dot_general x2, matrix products, forward_tiles(): jnp.einsum('tab,tbf->taf', tile_block, picked, precision=lax.Precision.HI...  46 us
    all_gather x1, waiting for transfers between devices, per_device(): rows_out = lax.all_gather(cotangent, 'col', axis=0, tiled=True)  42.2 us
    dot_general x2, local copies, waits for them, and re-layouts, forward_tiles(): jnp.einsum('tab,tbf->taf', tile_block, picked, precision=lax.Precision.HI...  23.3 us
  transfers between devices with their start and end apart: 9, of which 5 were waited for; matrix products, arithmetic and copies ran while one was open for 35% of the time, Pallas kernels for 0%

commit v1 on v0

--- a/solution.py
+++ b/solution.py
@@ -72,7 +72,7 @@
     adjoint_one = adjoint_tiles(rows_in, tile_row, tile_col, tile_block, col_tiles)
     d_support = lax.psum_scatter(adjoint_one, "row", scatter_dimension=0, tiled=True)
     grad_in_local = inner_rows(x_local, d_support)
-    grad_in, grad_out = lax.psum((grad_in_local, grad_out_local), ("row", "col"))
+    grad_in, grad_out = lax.psum(lax.psum((grad_in_local, grad_out_local), "col"), "row")
     return (output, grad_in, grad_out)
 
 

time: 653 us -> 644 us (0.986)
  waiting for transfers between devices: 384 us -> 375 us
    psum x1 -> x2, waiting for transfers between devices: 135 us -> 101 us  [the longest x1 50.8 us: per_device(): lax.psum(lax.psum((grad_in_local, grad_out_local), 'col'), 'row')]
    reduce_scatter x1, waiting for transfers between devices: 0.01 us -> 22.5 us  [per_device(): lax.psum_scatter(adjoint_one, 'row', scatter_dimension=0, tiled=True)]
  transfers between devices with their start and end apart: 9 -> 10, of which waited for: 5 -> 7; matrix products, arithmetic and copies ran while one was open for 35% -> 36% of each run, Pallas kernels for 0% -> 0%
where the time goes in v1:
time: 644 us; the launch traced here: 634 us
  waiting for transfers between devices  375 us (58%)
  matrix products  129 us (20%)
  local copies, waits for them, and re-layouts  104 us (16%)
  between operations  14.7 us (2%)
  blocking collectives  10.3 us (2%)
    reduce_scatter x1, waiting for transfers between devices, per_device(): lax.psum_scatter(partial_two, 'col', scatter_dimension=0, tiled=True)  80.2 us
    reduce_scatter x1, waiting for transfers between devices, per_device(): lax.psum_scatter(partial_one, 'col', scatter_dimension=0, tiled=True)  78.6 us
    psum x1, waiting for transfers between devices, per_device(): lax.psum(lax.psum((grad_in_local, grad_out_local), 'col'), 'row')  50.8 us
    psum x1, waiting for transfers between devices, per_device(): lax.psum((grad_in_local, grad_out_local), 'col')  50.7 us
    all_gather x1, waiting for transfers between devices, per_device(): rows_in = lax.all_gather(d_pre, 'col', axis=0, tiled=True)  48.8 us
    dot_general x2, matrix products, adjoint_tiles(): jnp.einsum('tba,tbf->taf', tile_block, picked, precision=lax.Precision.HI...  46.5 us
    dot_general x2, matrix products, forward_tiles(): jnp.einsum('tab,tbf->taf', tile_block, picked, precision=lax.Precision.HI...  46.1 us
    all_gather x1, waiting for transfers between devices, per_device(): rows_out = lax.all_gather(cotangent, 'col', axis=0, tiled=True)  42.2 us
  transfers between devices with their start and end apart: 10, of which 7 were waited for; matrix products, arithmetic and copies ran while one was open for 36% of the time, Pallas kernels for 0%

profile of v1, /device:TPU:0, one launch (start us, length us, event | category | flops | bytes accessed | tf_op | source)
XLA Modules:
  0.0 634.2 jit_solution(5591188312396909658)
XLA Ops:
  8.9 10.3 %all_to_all.19 = f32[8,256,16]{1,2,0:T(8,128)S(1)} all-to-all(f32[8,256,16]{1,2,0:T(8,128)S(1)} %bitcast.80), channel_id=1, replica_groups=mesh['row'=8,'col'=16] {'row'}, dimensions={0} | all-to-all | bytes 262144 | tf_op jit(solution)/shard_map/all_to_all | solution.py:54
  19.2 2.0 fusion.69
  22.0 42.2 %all-gather.9.cloned.1.call-done = f32[4096,256]{1,0:T(8,128)} async-done(((f32[256,256]{1,0:T(8,128)}), f32[4096,256]{1,0:T(8,128)}) %all-gather.9.cloned.1.call-update) | async-done | bytes 4194320 | tf_op jit(solution)/shard_map/all_gather | solution.py:64
  64.2 9.8 %gather_fusion.2 = f32[80,128,256]{2,1,0:T(8,128)} fusion(f32[32,128,256]{2,1,0:T(8,128)} %bitcast.72, s32[1024]{0:T(1024)S(1)} %pad_clamp_fusion), kind=kCustom, calls=%fused_computation.1.clone | custom fusion | bytes 20971840 | tf_op jit(solution)/shard_map/jit(_take)/gather | solution.py:25
  73.9 23.2 %fusion.30 = f32[80,128,256]{1,2,0:T(8,128)} fusion(f32[1,1,80,128,128]{4,3,2,1,0:T(8,128)} %param.14, f32[80,128,256]{2,1,0:T(8,128)} %gather_fusion.2, pred[80]{0:T(512)(128)(4,1)S(1)} %get-tuple-element.24), kind=kOutput, calls=%fused_computation.26 | convolution fusion | flops 4029153280 | bytes 26214480 | tf_op jit(solution)/shard_map/tba,tbf->taf/dot_general | solution.py:26
  97.1 11.7 %copy.48 = f32[80,128,256]{2,0,1:T(8,128)} copy(f32[80,128,256]{1,2,0:T(8,128)} %fusion.30) | data formatting | bytes 20971520 | tf_op jit(solution)/shard_map/tba,tbf->taf/dot_general | solution.py:26
  108.8 6.2 fusion.57
  115.0 2.5 copy.49
  118.1 9.8 %gather_fusion = f32[80,128,256]{2,1,0:T(8,128)} fusion(f32[16,128,256]{2,1,0:T(8,128)} %bitcast.70, s32[1024]{0:T(1024)S(1)} %pad_clamp_fusion.1), kind=kCustom, calls=%fused_computation.clone | custom fusion | bytes 20971840 | tf_op jit(solution)/shard_map/jit(_take)/gather | solution.py:12
  127.8 23.1 %fusion.20 = f32[80,128,256]{1,2,0:T(8,128)} fusion(f32[1,1,80,128,128]{4,3,2,1,0:T(8,128)} %param.14, f32[80,128,256]{2,1,0:T(8,128)} %gather_fusion, pred[80]{0:T(512)(128)(4,1)S(1)} %compare_and_fusion.1), kind=kOutput, calls=%fused_computation.24 | convolution fusion | flops 4029153280 | bytes 26214480 | tf_op jit(solution)/shard_map/tab,tbf->taf/dot_general | solution.py:13
  150.9 11.6 %copy.42 = f32[80,128,256]{2,0,1:T(8,128)} copy(f32[80,128,256]{1,2,0:T(8,128)} %fusion.20) | data formatting | bytes 20971520 | tf_op jit(solution)/shard_map/tab,tbf->taf/dot_general | solution.py:13
  162.6 6.9 %fusion.49 = f32[32,128,256]{2,0,1:T(8,128)S(1)} fusion(f32[80,128,256]{2,0,1:T(8,128)} %copy.42, s32[80]{0:T(128)S(1)} %bitcast.82), kind=kOutput, calls=%fused_computation.39 | convolution fusion | flops 1006635520 | bytes 14680384 | tf_op jit(solution)/shard_map/rt,taf->raf/dot_general | solution.py:17
  169.4 4.5 copy.43
  174.0 78.6 %reduce-scatter.5.cloned.1.call-done = f32[256,256]{1,0:T(8,128)} async-done(((f32[4096,256]{1,0:T(8,128)}), f32[256,256]{1,0:T(8,128)}) %reduce-scatter.5.cloned.1.call-update) | async-done | bytes 262160 | tf_op jit(solution)/shard_map/reduce_scatter | solution.py:58
  252.6 2.1 fusion.40
  254.8 2.1 fusion.44
  256.9 48.8 %all-gather.11.cloned.1.call-done = f32[4096,256]{1,0:T(8,128)} async-done(((f32[256,256]{1,0:T(8,128)}), f32[4096,256]{1,0:T(8,128)}) %all-gather.11.cloned.1.call-update) | async-done | bytes 4194320 | tf_op jit(solution)/shard_map/all_gather | solution.py:71
  305.8 10.0 %gather_fusion.3 = f32[80,128,256]{2,1,0:T(8,128)} fusion(f32[32,128,256]{2,1,0:T(8,128)} %bitcast.73, s32[1024]{0:T(1024)S(1)} %pad_clamp_fusion), kind=kCustom, calls=%fused_computation.3.clone | custom fusion | bytes 20971840 | tf_op jit(solution)/shard_map/jit(_take)/gather | solution.py:25
  315.8 23.3 %fusion.35 = f32[80,128,256]{1,2,0:T(8,128)} fusion(f32[1,1,80,128,128]{4,3,2,1,0:T(8,128)} %param.14, f32[80,128,256]{2,1,0:T(8,128)} %gather_fusion.3, pred[80]{0:T(512)(128)(4,1)S(1)} %get-tuple-element.24), kind=kOutput, calls=%fused_computation.27 | convolution fusion | flops 4029153280 | bytes 26214480 | tf_op jit(solution)/shard_map/tba,tbf->taf/dot_general | solution.py:26
  339.0 11.7 %copy.51 = f32[80,128,256]{2,0,1:T(8,128)} copy(f32[80,128,256]{1,2,0:T(8,128)} %fusion.35) | data formatting | bytes 20971520 | tf_op jit(solution)/shard_map/tba,tbf->taf/dot_general | solution.py:26
  350.7 6.3 fusion.55
  357.0 2.5 copy.52
  361.1 9.7 %gather_fusion.1 = f32[80,128,256]{2,1,0:T(8,128)} fusion(f32[16,128,256]{2,1,0:T(8,128)} %bitcast.71, s32[1024]{0:T(1024)S(1)} %pad_clamp_fusion.1), kind=kCustom, calls=%fused_computation.2.clone | custom fusion | bytes 20971840 | tf_op jit(solution)/shard_map/jit(_take)/gather | solution.py:12
  370.8 22.5 %reduce-scatter.11.cloned.1.call-done = f32[256,256]{1,0:T(8,128)} async-done(((f32[2048,256]{1,0:T(8,128)}), f32[256,256]{1,0:T(8,128)}) %reduce-scatter.11.cloned.1.call-update) | async-done | bytes 262160 | tf_op jit(solution)/shard_map/reduce_scatter | solution.py:73
  393.3 2.2 convolution_bitcast_fusion
  395.6 23.1 %fusion.25 = f32[80,128,256]{1,2,0:T(8,128)} fusion(f32[1,1,80,128,128]{4,3,2,1,0:T(8,128)} %param.14, f32[80,128,256]{2,1,0:T(8,128)} %gather_fusion.1, pred[80]{0:T(512)(128)(4,1)S(1)} %compare_and_fusion.1), kind=kOutput, calls=%fused_computation.25 | convolution fusion | flops 4029153280 | bytes 26214480 | tf_op jit(solution)/shard_map/tab,tbf->taf/dot_general | solution.py:13
  418.7 11.7 %copy.45 = f32[80,128,256]{2,0,1:T(8,128)} copy(f32[80,128,256]{1,2,0:T(8,128)} %fusion.25) | data formatting | bytes 20971520 | tf_op jit(solution)/shard_map/tab,tbf->taf/dot_general | solution.py:13
  430.3 50.7 %all-reduce.5.cloned.1.call-done = (f32[128,256]{0,1:T(8,128)}, f32[256,256]{1,0:T(8,128)}) async-done(((f32[128,256]{0,1:T(8,128)}, f32[256,256]{1,0:T(8,128)}), (f32[128,256]{0,1:T(8,128)}, f32[256,256]{1,0:T(8,128)})) %all-reduce.5.cloned.1.call-update) | async-done | bytes 393232 | tf_op jit(solution)/shard_map/psum | solution.py:75
  481.3 6.9 %fusion.47 = f32[32,128,256]{2,0,1:T(8,128)S(1)} fusion(f32[80,128,256]{2,0,1:T(8,128)} %copy.45, s32[80]{0:T(128)S(1)} %bitcast.83), kind=kOutput, calls=%fused_computation.38 | convolution fusion | flops 1006635520 | bytes 14680384 | tf_op jit(solution)/shard_map/rt,taf->raf/dot_general | solution.py:17
  488.2 4.4 copy.46
  492.6 50.8 %all-reduce.7.cloned.1.call-done = (f32[128,256]{0,1:T(8,128)}, f32[256,256]{1,0:T(8,128)}) async-done(((f32[128,256]{0,1:T(8,128)}, f32[256,256]{1,0:T(8,128)}), (f32[128,256]{0,1:T(8,128)}, f32[256,256]{1,0:T(8,128)})) %all-reduce.7.cloned.1.call-update) | async-done | bytes 393232 | tf_op jit(solution)/shard_map/psum | solution.py:75
  545.1 80.2 %reduce-scatter.7.cloned.1.call-done = f32[256,256]{1,0:T(8,128)} async-done(((f32[4096,256]{1,0:T(8,128)}), f32[256,256]{1,0:T(8,128)}) %reduce-scatter.7.cloned.1.call-update) | async-done | bytes 262160 | tf_op jit(solution)/shard_map/reduce_scatter | solution.py:63
  (44 shorter events, 8.4 us)
Async XLA Ops:
  7.2 245.4 %copy-start = (f32[256,256]{1,0:T(8,128)S(1)}, f32[256,256]{1,0:T(8,128)}, u32[]{:S(2)}) copy-start(f32[256,256]{1,0:T(8,128)} %param.16) | copy-start | bytes 786436
  7.2 57.0 %all-gather.9.cloned.1.call-start = ((), (), s32[]{:S(2)}) async-start(), calls=%async_computation.9 | async-start | bytes 4456448 | tf_op jit(solution)/shard_map/all_gather | solution.py:64
  7.9 110.1 %all-gather.5.cloned.1.call-start = ((), (), s32[]{:S(2)}) async-start(), calls=%async_computation.5 | async-start | bytes 2359296 | tf_op jit(solution)/shard_map/all_gather | solution.py:56
  21.2 152.7 %reduce-scatter.9.cloned.1.call-start = ((), (), s32[]{:S(2)}) async-start(), calls=%async_computation.10 | async-start | bytes 2359296 | tf_op jit(solution)/shard_map/reduce_scatter | solution.py:66
  97.1 11.7 %copy-start.3 = (s32[1,1,80]{2,1,0:T(1,128)S(1)}, s32[1,1,80]{2,1,0:T(1,128)}, u32[]{:S(2)}) copy-start(s32[1,1,80]{2,1,0:T(1,128)} %param.13) | copy-start | bytes 964
  117.6 135.0 %reduce-scatter.5.cloned.1.call-start = ((), (), s32[]{:S(2)}) async-start(), calls=%async_computation.6 | async-start | bytes 4456448 | tf_op jit(solution)/shard_map/reduce_scatter | solution.py:58
  150.9 11.6 %copy-start.2 = (s32[1,1,80]{2,1,0:T(1,128)S(1)}, s32[1,1,80]{2,1,0:T(1,128)}, u32[]{:S(2)}) copy-start(s32[1,1,80]{2,1,0:T(1,128)} %param.12) | copy-start | bytes 964
  173.9 131.8 %all-gather.11.cloned.1.call-start = ((), (), s32[]{:S(2)}) async-start(), calls=%async_computation.11 | async-start | bytes 4456448 | tf_op jit(solution)/shard_map/all_gather | solution.py:71
  254.7 106.4 %all-gather.7.cloned.1.call-start = ((), (), s32[]{:S(2)}) async-start(), calls=%async_computation.7 | async-start | bytes 2359296 | tf_op jit(solution)/shard_map/all_gather | solution.py:61
  256.9 136.4 %reduce-scatter.11.cloned.1.call-start = ((), (), s32[]{:S(2)}) async-start(), calls=%async_computation.12 | async-start | bytes 2359296 | tf_op jit(solution)/shard_map/reduce_scatter | solution.py:73
  350.7 9.1 %copy-start.4 = (f32[256,256]{1,0:T(8,128)S(1)}, f32[256,256]{1,0:T(8,128)}, u32[]{:S(2)}) copy-start(f32[256,256]{1,0:T(8,128)} %reduce-scatter.9.cloned.1.call-done) | copy-start | bytes 786436
  350.7 9.1 %copy-start.5 = (f32[256,256]{1,0:T(8,128)S(1)}, f32[256,256]{1,0:T(8,128)}, u32[]{:S(2)}) copy-start(f32[256,256]{1,0:T(8,128)} %reduce-scatter.5.cloned.1.call-done) | copy-start | bytes 786436
  359.5 121.5 %all-reduce.5.cloned.1.call-start = ((), (), s32[]{:S(2)}) async-start(), calls=%async_computation.13 | async-start | bytes 786432 | tf_op jit(solution)/shard_map/psum | solution.py:75
  395.5 147.9 %all-reduce.7.cloned.1.call-start = ((), (), s32[]{:S(2)}) async-start(), calls=%async_computation.14 | async-start | bytes 786432 | tf_op jit(solution)/shard_map/psum | solution.py:75
  481.0 145.9 %copy-start.1 = (f32[256,256]{1,0:T(8,128)S(1)}, f32[256,256]{1,0:T(8,128)}, u32[]{:S(2)}) copy-start(f32[256,256]{1,0:T(8,128)} %param.16) | copy-start | bytes 786436
  481.0 144.3 %reduce-scatter.7.cloned.1.call-start = ((), (), s32[]{:S(2)}) async-start(), calls=%async_computation.8 | async-start | bytes 4456448 | tf_op jit(solution)/shard_map/reduce_scatter | solution.py:63
Sparse Core Ops, SparseCore 0:
  10.1 53.9 all-gather.8
  66.5 24.8 all-gather.4
  117.7 33.6 reduce-scatter.8
  174.0 78.4 reduce-scatter.4
  255.1 50.5 all-gather.10
  307.9 24.8 all-gather.6
  359.6 33.6 reduce-scatter.10
  397.2 83.7 all-reduce.4
  483.4 59.9 all-reduce.6
  547.2 78.0 reduce-scatter.6
